TPU v7x, 256 devices: a whole 4x4x8 slice. The times are simulated.
256 devices in a mesh: blk: 8 (over y, x_hi), ctx: 32 (over z, x_lo, core).
Axes of the slice: x: 4 (x_hi: 2, x_lo: 2; x = x_hi * 2 + x_lo), y: 4, z: 8, core: 2. Of those that a mesh axis runs over, the one named last changes fastest.
Arguments:
- tokens: bfloat16 [8, 4096, 1024], P('blk', 'ctx'), may hold values from -16 to 16
- segment_ids: int32 [8, 4096], P('blk', 'ctx'), may hold values from 0 to 3, never falling along the last dimension, each value on 1 to 3072 neighbouring positions
- norm_gain: bfloat16 [8, 2, 1024], P('blk'), may hold values from 0.25 to 1.75
- w_mamba_in: bfloat16 [8, 1024, 2048], P('blk', None, 'ctx'), may hold values from -0.1875 to 0.1875
- w_ssm_param: bfloat16 [8, 1024, 160], P('blk'), may hold values from -0.1875 to 0.1875
- ssm_rate: bfloat16 [8, 32], P('blk'), may hold values from 7.2956085e-05 to 0.059814453
- dt_bias: bfloat16 [8, 32], P('blk'), may hold values from -1 to 1
- skip_gain: bfloat16 [8, 32], P('blk'), may hold values from 0.5 to 1.5
- ssm_norm_gain: bfloat16 [8, 2048], P('blk'), may hold values from 0.25 to 1.75
- w_mamba_out: bfloat16 [8, 2048, 1024], P('blk', 'ctx'), may hold values from -0.125 to 0.125
- w_qkv: bfloat16 [8, 1024, 2048], P('blk', None, 'ctx'), may hold values from -1.5 to 1.5
- w_attn_out: bfloat16 [8, 1024, 1024], P('blk', 'ctx'), may hold values from -0.75 to 0.75
Outputs:
- layer_out: bfloat16 [8, 4096, 1024], P('blk', 'ctx')
Inputs may be any that keep to these rules, and one draw needn't show every extreme that they name: `segment_ids`: within each micro-batch the ids never fall along the sequence; each document holds 1 to 3072 tokens, and one holds exactly that many.
All inputs are finite; a program needn't handle non-finite values.
Results may differ from a plain program's by a relative error of at most 0.015.
Values may be sent and summed in bfloat16 or wider, within the bound.
No kernel may reach another device: no remote copies, remote signals or barrier semaphores. Data moves between devices by JAX's collectives and lax.ppermute only.
A program may use at most 128 MiB of HBM per device.

v0:
```python
import math
import jax
import jax.numpy as jnp
from jax import lax
from jax.sharding import Mesh
from jax.sharding import PartitionSpec as P

INNER = 2048
HEAD_DIM = 64
STATE = 64
QUERY_HEADS = 8
KV_HEADS = 4
ATTN_DIM = 128
SPAN = 64
CTX = ("ctx_0", "ctx_1", "ctx_2")
epsilon = 1e-05
highest = lax.Precision.HIGHEST


def filled_with(value, identity):
    return jax.tree.map(
        lambda part, zero: jnp.zeros_like(part) + jnp.asarray(zero, part.dtype), value, identity
    )


def gathered_once(value, axis):
    leaves = jax.tree.leaves(value)
    turns = sorted(range(len(leaves)), key=lambda k: -leaves[k].size)
    width = (1, *leaves[turns[0]].shape)[-1]
    lines = [
        jnp.pad(leaves[k].reshape(-1), (0, -leaves[k].size % width)).reshape(-1, width)
        for k in turns
    ]
    both, at, found = (lax.all_gather(jnp.concatenate(lines), axis), 0, {})
    for k, line in zip(turns, lines):
        slab = both[:, at : at + len(line)].reshape(len(both), -1)
        found[k] = slab[:, : leaves[k].size].reshape(-1, *leaves[k].shape)
        at += len(line)
    numbers = iter(range(len(leaves)))
    return jax.tree.map(lambda _: found[next(numbers)], value)


def collected_alike(value, axis):
    leaves, found = (jax.tree.leaves(value), {})
    for initial, a in enumerate(leaves):
        if initial not in found:
            alike = [k for k, b in enumerate(leaves) if b.dtype == a.dtype]
            got = (
                gathered_once([leaves[k] for k in alike], axis)
                if len(alike) > 1
                else [lax.all_gather(a, axis)]
            )
            for k, b in zip(alike, got):
                found[k] = b
    numbers = iter(range(len(leaves)))
    return jax.tree.map(lambda _: found[next(numbers)], value)


def entering_2(value, axes, combine, identity):
    before = start = filled_with(value, identity)
    so_far = value
    for axis in reversed(axes):
        size, mine = (lax.axis_size(axis), lax.axis_index(axis))
        pieces = collected_alike(so_far, axis)
        inside, so_far = (start, start)
        for k in range(size):
            passed = k < mine
            so_far = combine(so_far, jax.tree.map(lambda part: part[k], pieces))
            inside = jax.tree.map(lambda new, old: jnp.where(passed, new, old), so_far, inside)
        before = combine(inside, before)
    return before


def joined_along(blocks, dim):
    dims = list(blocks.shape[1:])
    dims[dim] *= blocks.shape[0]
    return jnp.moveaxis(blocks, 0, dim).reshape(dims)


def all_blocks(value, axes, turns):
    blocks = value
    for k in turns:
        blocks = lax.all_gather(blocks, axes[k])
    done = turns[::-1]
    back = [done.index(k) for k in range(len(axes))]
    blocks = blocks.transpose(*back, *range(len(axes), blocks.ndim))
    return blocks.reshape(-1, *value.shape)


def whole_of(value, axes, turns, dim):
    return joined_along(all_blocks(value, axes, turns), dim)


def in_one_piece(arrays, axis, dim, along):
    ends, at = ([], 0)
    for a in arrays[:-1]:
        at += a.shape[along]
        ends.append(at)
    both = jnp.concatenate(arrays, axis=along)
    return tuple(jnp.split(lax.all_gather(both, axis, axis=dim, tiled=True), ends, axis=along))


def from_behind(value, axis, steps):
    count = lax.axis_size(axis)
    pairs = [(source, (source + steps) % count) for source in range(count)]
    return lax.ppermute(value, axis, pairs)


def rms_norm(values, gain):
    values = values.astype(jnp.float32)
    scale = lax.rsqrt(jnp.mean(values * values, axis=-1, keepdims=True) + epsilon)
    return values * scale * gain.astype(jnp.float32)


def span_update(carry, block):
    state, prev_segment = carry
    inner_value, bin_value, cout_value, delta, log_decay, segment = block
    cumul = jnp.cumsum(log_decay, axis=0)
    order = jnp.arange(segment.shape[0])
    allowed = (order[:, None] >= order[None, :]) & (segment[:, None] == segment[None, :])
    differ = cumul[:, None, :] - cumul[None, :, :]
    factor = jnp.where(allowed[:, :, None], jnp.exp(jnp.minimum(differ, 0.0)), 0.0)
    intersection = jnp.dot(cout_value, bin_value.T, precision=highest)
    mixing = factor * intersection[:, :, None] * delta[None, :, :]
    within = jnp.einsum("tsh,shp->thp", mixing, inner_value, precision=highest)
    carried = jnp.where((segment == prev_segment)[:, None], jnp.exp(cumul), 0.0)
    across = jnp.einsum("tn,hpn->thp", cout_value, state, precision=highest) * carried[:, :, None]
    last_segment = segment[-1]
    keeping = (
        jnp.where((segment == last_segment)[:, None], jnp.exp(cumul[-1][None, :] - cumul), 0.0)
        * delta
    )
    fresh = jnp.einsum("sh,shp,sn->hpn", keeping, inner_value, bin_value, precision=highest)
    passing = jnp.where(prev_segment == last_segment, jnp.exp(cumul[-1]), 0.0)
    state = passing[:, None, None] * state + fresh
    return ((state, last_segment), within + across)


def combine_states(earlier, later):
    early_first, early_last, early_pass, early_state = earlier
    late_first, late_last, late_pass, late_state = later
    joined = (late_first == early_last) | (early_last < 0) | (late_first < 0)
    factor = jnp.where(joined, late_pass, 0.0)
    first = jnp.where(early_first < 0, late_first, early_first)
    last = jnp.where(late_last < 0, early_last, late_last)
    return (first, last, early_pass * factor, factor[:, None, None] * early_state + late_state)


def layer_pair(tokens, segment, weights):
    (
        norm_gain,
        w_mamba_in,
        w_ssm_param,
        ssm_rate,
        dt_bias,
        skip_gain,
        ssm_norm_gain,
        w_mamba_out,
        w_qkv,
        w_attn_out,
    ) = weights
    rows = tokens.shape[0]
    heads = ssm_rate.shape[0]
    offset = lax.axis_index(CTX) * rows
    normed = rms_norm(tokens, norm_gain[0]).astype(jnp.bfloat16)
    inner = jnp.dot(
        normed,
        lax.all_gather(w_mamba_in, CTX, axis=1, tiled=True),
        preferred_element_type=jnp.float32,
    ).astype(jnp.bfloat16)
    params = jnp.dot(normed, w_ssm_param, preferred_element_type=jnp.float32)
    bin_value = params[:, :STATE]
    cout_value = params[:, STATE : 2 * STATE]
    delta = jax.nn.softplus(params[:, 2 * STATE :] + dt_bias.astype(jnp.float32))
    log_decay = -delta * ssm_rate.astype(jnp.float32)
    inner_value = inner.astype(jnp.float32).reshape(rows, heads, HEAD_DIM)
    blocks = tuple(
        (
            item.reshape((rows // SPAN, SPAN) + item.shape[1:])
            for item in (inner_value, bin_value, cout_value, delta, log_decay, segment)
        )
    )
    start_carry = (jnp.zeros((heads, HEAD_DIM, STATE), jnp.float32), segment[0])
    (local_state, ignored), mixed = lax.scan(span_update, start_carry, blocks)
    device_decay = jnp.cumsum(log_decay, axis=0)
    through = jnp.where(segment[0] == segment[-1], jnp.exp(device_decay[-1]), 0.0)
    element = (segment[0], segment[-1], through, local_state)
    identity = (
        jnp.array(-1, jnp.int32),
        jnp.array(-1, jnp.int32),
        jnp.ones_like(through),
        jnp.zeros_like(local_state),
    )
    scanned = entering_2(element, CTX, combine_states, identity)
    incoming_segment = scanned[1]
    incoming_state = scanned[3]
    linked = jnp.where((segment == incoming_segment)[:, None], jnp.exp(device_decay), 0.0)
    entering = (
        jnp.einsum("tn,hpn->thp", cout_value, incoming_state, precision=highest)
        * linked[:, :, None]
    )
    mixed = (
        mixed.reshape(rows, heads, HEAD_DIM)
        + entering
        + skip_gain.astype(jnp.float32)[None, :, None] * inner_value
    )
    ssm_out = rms_norm(mixed.reshape(rows, INNER), ssm_norm_gain).astype(jnp.bfloat16)
    columns = ssm_out
    first = tokens.astype(jnp.float32) + jnp.dot(
        columns, whole_of(w_mamba_out, CTX, (1, 0, 2), 0), preferred_element_type=jnp.float32
    )
    hidden = rms_norm(first, norm_gain[1]).astype(jnp.bfloat16)
    projected = jnp.dot(
        hidden, lax.all_gather(w_qkv, CTX, axis=1, tiled=True), preferred_element_type=jnp.float32
    ).astype(jnp.bfloat16)
    groups = QUERY_HEADS // KV_HEADS
    query = projected[:, : QUERY_HEADS * ATTN_DIM].reshape(rows, KV_HEADS, groups, ATTN_DIM)
    keys = projected[:, QUERY_HEADS * ATTN_DIM : (QUERY_HEADS + KV_HEADS) * ATTN_DIM]
    values = projected[:, (QUERY_HEADS + KV_HEADS) * ATTN_DIM :]
    positions = offset + jnp.arange(rows)
    scale = 1.0 / math.sqrt(ATTN_DIM)
    top = jnp.full((KV_HEADS, groups, rows), -1e30, jnp.float32)
    key_piece, value_piece, segment_piece = (
        *in_one_piece((keys, values), CTX, 0, 1),
        lax.all_gather(segment, CTX, axis=0, tiled=True),
    )
    count = key_piece.shape[0]
    key_position = jnp.arange(count)
    scores = (
        jnp.einsum(
            "tkgd,skd->kgts",
            query,
            key_piece.reshape(count, KV_HEADS, ATTN_DIM),
            preferred_element_type=jnp.float32,
        )
        * scale
    )
    allowed = (key_position[None, :] <= positions[:, None]) & (
        segment_piece[None, :] == segment[:, None]
    )
    scores = jnp.where(allowed, scores, -1e30)
    new_top = jnp.maximum(top, jnp.max(scores, axis=-1))
    probs = jnp.where(allowed, jnp.exp(scores - new_top[..., None]), 0.0)
    total = jnp.sum(probs, axis=-1)
    attend_context = jnp.einsum(
        "kgts,skd->kgtd",
        probs.astype(jnp.bfloat16),
        value_piece.reshape(count, KV_HEADS, ATTN_DIM),
        preferred_element_type=jnp.float32,
    )
    top, total, context = (new_top, total, attend_context)
    context = context / total[..., None]
    context = (
        jnp.transpose(context, (2, 0, 1, 3))
        .reshape(rows, QUERY_HEADS * ATTN_DIM)
        .astype(jnp.bfloat16)
    )
    columns = context
    result = first + jnp.dot(
        columns,
        lax.all_gather(w_attn_out, CTX, axis=0, tiled=True),
        preferred_element_type=jnp.float32,
    )
    return result.astype(jnp.bfloat16)


def on_device(
    tokens,
    segment_ids,
    norm_gain,
    w_mamba_in,
    w_ssm_param,
    ssm_rate,
    dt_bias,
    skip_gain,
    ssm_norm_gain,
    w_mamba_out,
    w_qkv,
    w_attn_out,
):
    arrived = from_behind(
        (
            norm_gain,
            w_mamba_in,
            w_ssm_param,
            ssm_rate,
            dt_bias,
            skip_gain,
            ssm_norm_gain,
            w_mamba_out,
            w_qkv,
            w_attn_out,
        ),
        "blk",
        1,
    )
    section = tuple((item[0] for item in arrived))
    result = layer_pair(tokens[0], segment_ids[0], section)
    return result[None]


def solution(mesh):
    finer = Mesh(
        mesh.devices.reshape(mesh.shape["blk"], 8, 2, 2), ("blk", "ctx_0", "ctx_1", "ctx_2")
    )
    in_specs = (
        P("blk", CTX, None),
        P("blk", CTX),
        P("blk", None, None),
        P("blk", None, CTX),
        P("blk", None, None),
        P("blk", None),
        P("blk", None),
        P("blk", None),
        P("blk", None),
        P("blk", CTX, None),
        P("blk", None, CTX),
        P("blk", CTX, None),
    )
    out_specs = P("blk", CTX, None)
    return jax.shard_map(
        on_device, mesh=finer, in_specs=in_specs, out_specs=out_specs, check_vma=False
    )
```

profile of v0, /device:TPU:1, one launch (start us, length us, event | category | flops | bytes accessed | tf_op | source)
XLA Modules:
  0.0 555.6 jit_solution(135234453946944221)
XLA Ops:
  10.1 5.0 collective-permute-done.4
  34.9 50.0 %all-gather.27.cloned.1.call-done = bf16[1,1024,2048]{1,2,0:T(8,128)(2,1)} async-done(((bf16[1,1024,64]{1,2,0:T(8,128)(2,1)}), bf16[1,1024,2048]{1,2,0:T(8,128)(2,1)}) %all-gather.27.cloned.1.call-update) | async-done | bytes 4194320 | tf_op jit(solution)/shard_map/all_gather | solution.py:168
  84.8 3.8 fusion.48
  90.8 76.6 %while.15 = (s32[]{:T(128)}, f32[32,64,64]{2,1,0:T(8,128)S(1)}, s32[]{:T(128)}, f32[2,64,32,64]{1,0,3,2:T(2,128)}, s32[2,64]{1,0:T(2,128)}, /*index=5*/f32[2,64,...) while((s32[]{:T(128)}, f32[32,64,64]{2,1,0:T(8,128)S(1)}, ...), condition=%wide.region_3.4_spmd.clone, body=%wide.region_1.3_spmd.clone.sunk | while | flops 306858144 | bytes 9277010 | solution.py:184
  103.0 25.4 %dynamic_update_slice.6 = f32[2,64,32,64]{1,0,3,2:T(2,128)} dynamic-update-slice(f32[2,64,32,64]{1,0,3,2:T(2,128)} %get-tuple-element.314, f32[1,64,32,64]{1,0,3,2:T(1,128)S(1)} %bitcast.295, s32[]{:T(128)S(6)} %copy.185, s32[]{:T(128)} %constant.29.clone.1..sunk, s32[]{:T(128)} %constant.29.clone.1..sunk, s32[]{:T(128)} %constant.29.clone.1..sunk) | dynamic-update-slice | bytes 1048580 | tf_op jit(solution)/shard_map/while/body/jit(dynamic_update_index_in_dim)/dynamic_update_slice | solution.py:184
  141.3 25.4 %dynamic_update_slice.6 = f32[2,64,32,64]{1,0,3,2:T(2,128)} dynamic-update-slice(f32[2,64,32,64]{1,0,3,2:T(2,128)} %get-tuple-element.314, f32[1,64,32,64]{1,0,3,2:T(1,128)S(1)} %bitcast.295, s32[]{:T(128)S(6)} %copy.185, s32[]{:T(128)} %constant.29.clone.1..sunk, s32[]{:T(128)} %constant.29.clone.1..sunk, s32[]{:T(128)} %constant.29.clone.1..sunk) | dynamic-update-slice | bytes 1048580 | tf_op jit(solution)/shard_map/while/body/jit(dynamic_update_index_in_dim)/dynamic_update_slice | solution.py:184
  172.1 6.0 %collective-permute-done.7 = bf16[1,64,1024]{2,1,0:T(8,128)(2,1)S(1)} collective-permute-done((bf16[1,64,1024]{2,1,0:T(8,128)(2,1)}, bf16[1,64,1024]{2,1,0:T(8,128)(2,1)S(1)}, u32[]{:S(2)}, u32[]{:S(2)}) %collective-permute-start.7) | collective-permute-done | bytes 131104 | tf_op jit(solution)/shard_map/ppermute | solution.py:106
  178.1 4.6 all_gather.79
  197.2 26.3 %all-gather.29.cloned.1.call-done = bf16[16,64,1024]{2,1,0:T(8,128)(2,1)} async-done(((bf16[2,64,1024]{2,1,0:T(8,128)(2,1)}), bf16[16,64,1024]{2,1,0:T(8,128)(2,1)}) %all-gather.29.cloned.1.call-update) | async-done | bytes 2097168 | tf_op jit(solution)/shard_map/all_gather | solution.py:83
  239.5 8.9 %all-reduce.5 = s32[16]{0:T(128)S(1)} all-reduce(s32[16]{0:T(128)S(1)} %fusion.174), channel_id=5, replica_groups=mesh['blk'=8,'ctx_0'=8,'ctx_1'=2,'ctx_2'=2] {'ctx_0'}, use_global_device_ids=true, to_apply=%add.5 | all-reduce | flops 16 | bytes 128
  267.0 4.7 collective-permute-done.8
  284.3 4.9 copy.121
  299.7 37.0 %all-gather.41.cloned.1.call-done = f32[8,2049,64]{1,2,0:T(8,128)} async-done(((f32[1,2049,64]{1,2,0:T(8,128)}), f32[8,2049,64]{1,2,0:T(8,128)}) %all-gather.41.cloned.1.call-update) | async-done | bytes 4196368 | tf_op jit(solution)/shard_map/all_gather | solution.py:34
  356.5 6.6 %multiply_reduce_fusion = (f32[128]{0:T(128)S(1)}, f32[128,32,64]{0,2,1:T(8,128)S(1)}) fusion(f32[32]{0:T(128)S(1)} %bitcast_convert_fusion, f32[128,2048]{0,1:T(8,128)S(1)} %copy.120, f32[128,32,64]{0,2,1:T(8,128)S(1)} %copy-done.5, f32[128,32]{0,1:T(8,128)S(1)} %exponential_select_fusion.2, f32[32,64,64]{2,1,0:T(8,128)} %bitcast.297, ...), kind=kOutput, calls=%fused_computation.76 | convolution fusion | flops 207748992 | bytes 15780236 | tf_op jit(solution)/shard_map/tn,hpn->thp/dot_general | solution.py:199
  364.5 39.8 %all-gather.33.cloned.1.call-done = bf16[1,1024,2048]{1,2,0:T(8,128)(2,1)} async-done(((bf16[1,1024,64]{1,2,0:T(8,128)(2,1)}), bf16[1,1024,2048]{1,2,0:T(8,128)(2,1)}) %all-gather.33.cloned.1.call-update) | async-done | bytes 4194320 | tf_op jit(solution)/shard_map/all_gather | solution.py:214
  411.3 32.5 %all-gather.9 = s32[1,4096]{1,0:T(1,128)S(1)} all-gather(s32[1,128]{1,0:T(1,128)S(1)} %copy-done.12), channel_id=11, replica_groups=mesh['blk'=8,'ctx_0'=8,'ctx_1'=2,'ctx_2'=2] {'ctx_0','ctx_1','ctx_2'}, dimensions={1}, use_global_device_ids=true | all-gather | bytes 16896 | tf_op jit(solution)/shard_map/all_gather | solution.py:225
  446.5 33.9 %all-gather.25.cloned.1.call-done = bf16[4096,1024]{1,0:T(8,128)(2,1)} async-done(((bf16[128,1024]{1,0:T(8,128)(2,1)}), bf16[4096,1024]{1,0:T(8,128)(2,1)}) %all-gather.25.cloned.1.call-update) | async-done | bytes 8388624 | tf_op jit(solution)/shard_map/all_gather | solution.py:100
  480.3 5.8 %fusion.182 = (bf16[4096,512]{1,0:T(8,128)(2,1)}, bf16[4096,512]{1,0:T(8,128)(2,1)}) fusion(bf16[4096,1024]{1,0:T(8,128)(2,1)} %all-gather.25.cloned.1.call-done), kind=kLoop, calls=%fused_computation.239 | loop fusion | bytes 16777216 | tf_op jit(solution)/shard_map/split | solution.py:100
  486.1 7.0 %reshape.498 = bf16[4096,4,128]{2,1,0:T(4,128)(2,1)} reshape(bf16[4096,512]{1,0:T(8,128)(2,1)} %get-tuple-element.166) | data formatting | bytes 8388608 | tf_op jit(solution)/shard_map/reshape | solution.py:233
  493.1 9.8 %fusion.33 = (f32[4,2,128]{2,1,0:T(2,128)S(1)}, f32[4,4096,128,2]{2,1,3,0:T(8,128)}) fusion(pred[128,4096]{0,1:T(8,128)(4,1)S(1)} %fusion.56, bf16[128,4,2,128]{3,2,1,0:T(2,128)(2,1)S(1)} %reshape.499, bf16[4096,4,128,1]{2,1,0,3:T(4,128)(2,1)} %bitcast.311), kind=kOutput, calls=%fused_computation.50 | convolution fusion | flops 1086323712 | bytes 21762048 | tf_op jit(solution)/shard_map/tkgd,skd->kgts/dot_general | solution.py:230
  502.9 6.5 %copy.149 = bf16[4096,512]{0,1:T(8,128)(2,1)} copy(bf16[4096,512]{1,0:T(8,128)(2,1)} %get-tuple-element.167) | data formatting | bytes 8388608 | tf_op jit(solution)/shard_map/reshape | solution.py:248
  509.3 8.2 %fusion.34 = f32[4,2,128]{2,1,0:T(2,128)S(1)} fusion(f32[4,4096,128,2]{2,1,3,0:T(8,128)} %get-tuple-element.226, f32[4,2,128]{2,1,0:T(2,128)S(1)} %broadcast_maximum_fusion, pred[128,4096]{0,1:T(8,128)(4,1)S(1)} %fusion.56), kind=kLoop, calls=%fused_computation.51 | loop fusion | flops 20970496 | bytes 17309696 | tf_op jit(solution)/shard_map/reduce_sum | solution.py:244
  520.1 6.5 %fusion.110 = bf16[128,4,2,128]{0,3,2,1:T(8,128)(2,1)S(1)} fusion(bf16[4096,4,128,1]{0,2,3,1:T(8,128)(2,1)} %bitcast.310, f32[4,4096,128,2]{2,1,3,0:T(8,128)S(1)} %copy-done, f32[4,2,128]{2,1,0:T(2,128)S(1)} %broadcast_maximum_fusion, pred[128,4096]{0,1:T(8,128)(4,1)S(1)} %fusion.56, f32[128,4,2]{0,2,1:T(2,128)S(1)} %bitcast.326), kind=kOutput, calls=%fused_computation.116 | convolution fusion | flops 1094975488 | bytes 21766144 | tf_op jit(solution)/shard_map/kgts,skd->kgtd/dot_general | solution.py:245
  526.6 19.5 %all-gather.35.cloned.1.call-done = bf16[1,1024,1024]{2,1,0:T(8,128)(2,1)} async-done(((bf16[1,32,1024]{2,1,0:T(8,128)(2,1)}), bf16[1,1024,1024]{2,1,0:T(8,128)(2,1)}) %all-gather.35.cloned.1.call-update) | async-done | bytes 2097168 | tf_op jit(solution)/shard_map/all_gather | solution.py:261
  (215 shorter events, 125.0 us)
Async XLA Ops:
  6.5 78.3 %all-gather.27.cloned.1.call-start = ((), (), s32[]{:S(2)}) async-start(), calls=%async_computation.1 | async-start | bytes 4325376 | tf_op jit(solution)/shard_map/all_gather | solution.py:168
  6.5 8.6 %collective-permute-start.4 = (bf16[1,1024,64]{1,2,0:T(8,128)(2,1)}, bf16[1,1024,64]{1,2,0:T(8,128)(2,1)S(1)}, u32[]{:S(2)}, u32[]{:S(2)}) collective-permute-start(bf16[1,1024,64]{1,2,0:T(8,128)(2,1)} %param.17), channel_id=1, source_target_pairs={{0,32},{32,64},{64,96},{96,128},{128,160},{160,192},{192,224},{224... | collective-permute-start | bytes 393224 | tf_op jit(solution)/shard_map/ppermute | solution.py:106
  15.8 177.7 %all-gather.37.cloned.1.call-start = ((), (), s32[]{:S(2)}) async-start(), calls=%async_computation.6 | async-start | bytes 1671168 | tf_op jit(solution)/shard_map/all_gather | solution.py:34
  15.8 14.6 %collective-permute-start = (bf16[1,2,1024]{2,1,0:T(2,128)(2,1)}, bf16[1,2,1024]{2,1,0:T(2,128)(2,1)S(1)}, u32[]{:S(2)}, u32[]{:S(2)}) collective-permute-start(bf16[1,2,1024]{2,1,0:T(2,128)(2,1)} %param.16), channel_id=1, source_target_pairs={{0,32},{32,64},{64,96},{96,128},{128,160},{160,192},{192,224},{224... | collective-permute-start | bytes 12296 | tf_op jit(solution)/shard_map/ppermute | solution.py:106
  17.0 13.4 %collective-permute-start.3 = (bf16[1,32]{1,0:T(2,128)(2,1)}, bf16[1,32]{1,0:T(2,128)(2,1)S(1)}, u32[]{:S(2)}, u32[]{:S(2)}) collective-permute-start(bf16[1,32]{1,0:T(2,128)(2,1)} %param.19), channel_id=1, source_target_pairs={{0,32},{32,64},{64,96},{96,128},{128,160},{160,192},{192,224},{224... | collective-permute-start | bytes 200 | tf_op jit(solution)/shard_map/ppermute | solution.py:106
  19.1 11.3 %collective-permute-start.2 = (bf16[1,32]{1,0:T(2,128)(2,1)}, bf16[1,32]{1,0:T(2,128)(2,1)S(1)}, u32[]{:S(2)}, u32[]{:S(2)}) collective-permute-start(bf16[1,32]{1,0:T(2,128)(2,1)} %param.20), channel_id=1, source_target_pairs={{0,32},{32,64},{64,96},{96,128},{128,160},{160,192},{192,224},{224... | collective-permute-start | bytes 200 | tf_op jit(solution)/shard_map/ppermute | solution.py:106
  21.0 11.2 %collective-permute-start.1 = (bf16[1,1024,160]{1,2,0:T(8,128)(2,1)}, bf16[1,1024,160]{1,2,0:T(8,128)(2,1)S(1)}, u32[]{:S(2)}, u32[]{:S(2)}) collective-permute-start(bf16[1,1024,160]{1,2,0:T(8,128)(2,1)} %param.18), channel_id=1, source_target_pairs={{0,32},{32,64},{64,96},{96,128},{128,160},{160,192},{192,224},{224... | collective-permute-start | bytes 983048 | tf_op jit(solution)/shard_map/ppermute | solution.py:106
  167.7 67.1 %copy-start.17 = (u32[256]{0:T(256)S(1)}, u32[256]{0:T(256)}, u32[]{:S(2)}) copy-start(u32[256]{0:T(256)} %constant.114) | copy-start | bytes 3076
  169.4 54.1 %all-gather.29.cloned.1.call-start = ((), (), s32[]{:S(2)}) async-start(), calls=%async_computation.2 | async-start | bytes 2359296 | tf_op jit(solution)/shard_map/all_gather | solution.py:83
  169.4 8.7 %collective-permute-start.7 = (bf16[1,64,1024]{2,1,0:T(8,128)(2,1)}, bf16[1,64,1024]{2,1,0:T(8,128)(2,1)S(1)}, u32[]{:S(2)}, u32[]{:S(2)}) collective-permute-start(bf16[1,64,1024]{2,1,0:T(8,128)(2,1)} %param.23), channel_id=1, source_target_pairs={{0,32},{32,64},{64,96},{96,128},{128,160},{160,192},{192,224},{224... | collective-permute-start | bytes 393224 | tf_op jit(solution)/shard_map/ppermute | solution.py:106
  182.7 77.8 %all-gather.39.cloned.1.call-start = ((), (), s32[]{:S(2)}) async-start(), calls=%async_computation.7 | async-start | bytes 1671168 | tf_op jit(solution)/shard_map/all_gather | solution.py:34
  194.9 69.2 %copy-start.13 = (bf16[1,1024,64]{1,2,0:T(8,128)(2,1)S(1)}, bf16[1,1024,64]{1,2,0:T(8,128)(2,1)}, u32[]{:S(2)}) copy-start(bf16[1,1024,64]{1,2,0:T(8,128)(2,1)} %param.24) | copy-start | bytes 393220
  196.2 76.3 %copy-start.15 = (bf16[1,2048]{1,0:T(2,128)(2,1)S(1)}, bf16[1,2048]{1,0:T(2,128)(2,1)}, u32[]{:S(2)}) copy-start(bf16[1,2048]{1,0:T(2,128)(2,1)} %param.22) | copy-start | bytes 12292
  196.2 77.0 %copy-start.16 = (bf16[1,32]{1,0:T(2,128)(2,1)S(1)}, bf16[1,32]{1,0:T(2,128)(2,1)}, u32[]{:S(2)}) copy-start(bf16[1,32]{1,0:T(2,128)(2,1)} %param.21) | copy-start | bytes 196
  196.2 87.8 %copy-start.12 = (s32[1,128]{1,0:T(1,128)S(1)}, s32[1,128]{1,0:T(1,128)}, u32[]{:S(2)}) copy-start(s32[1,128]{1,0:T(1,128)} %param.15) | copy-start | bytes 1540
  197.1 87.2 %all-gather.31.cloned.1.call-start = ((), (), s32[]{:S(2)}) async-start(), calls=%async_computation.3 | async-start | bytes 6291456 | tf_op jit(solution)/shard_map/all_gather | solution.py:83
  223.5 113.2 %all-gather.41.cloned.1.call-start = ((), (), s32[]{:S(2)}) async-start(), calls=%async_computation.8 | async-start | bytes 5013504 | tf_op jit(solution)/shard_map/all_gather | solution.py:34
  264.0 140.2 %all-gather.33.cloned.1.call-start = ((), (), s32[]{:S(2)}) async-start(), calls=%async_computation.4 | async-start | bytes 4325376 | tf_op jit(solution)/shard_map/all_gather | solution.py:214
  264.1 7.7 %collective-permute-start.8 = (bf16[1,1024,64]{1,2,0:T(8,128)(2,1)S(1)}, bf16[1,1024,64]{1,2,0:T(8,128)(2,1)S(1)}, u32[]{:S(2)}, u32[]{:S(2)}) collective-permute-start(bf16[1,1024,64]{1,2,0:T(8,128)(2,1)S(1)} %copy-done.13), channel_id=1, source_target_pairs={{0,32},{32,64},{64,96},{96,128},{128,160},{160,192},{192,224},{224... | collective-permute-start | bytes 393224 | tf_op jit(solution)/shard_map/ppermute | solution.py:106
  272.4 207.9 %all-gather.25.cloned.1.call-start = ((), (), s32[]{:S(2)}) async-start(), calls=%async_computation | async-start | bytes 8650752 | tf_op jit(solution)/shard_map/all_gather | solution.py:100
  272.5 11.6 %collective-permute-start.6 = (bf16[1,2048]{1,0:T(2,128)(2,1)S(1)}, bf16[1,2048]{1,0:T(2,128)(2,1)S(1)}, u32[]{:S(2)}, u32[]{:S(2)}) collective-permute-start(bf16[1,2048]{1,0:T(2,128)(2,1)S(1)} %copy-done.15), channel_id=1, source_target_pairs={{0,32},{32,64},{64,96},{96,128},{128,160},{160,192},{192,224},{224... | collective-permute-start | bytes 12296 | tf_op jit(solution)/shard_map/ppermute | solution.py:106
  273.1 10.9 %collective-permute-start.5 = (bf16[1,32]{1,0:T(2,128)(2,1)S(1)}, bf16[1,32]{1,0:T(2,128)(2,1)S(1)}, u32[]{:S(2)}, u32[]{:S(2)}) collective-permute-start(bf16[1,32]{1,0:T(2,128)(2,1)S(1)} %copy-done.16), channel_id=1, source_target_pairs={{0,32},{32,64},{64,96},{96,128},{128,160},{160,192},{192,224},{224... | collective-permute-start | bytes 200 | tf_op jit(solution)/shard_map/ppermute | solution.py:106
  408.7 137.4 %all-gather.35.cloned.1.call-start = ((), (), s32[]{:S(2)}) async-start(), calls=%async_computation.5 | async-start | bytes 2162688 | tf_op jit(solution)/shard_map/all_gather | solution.py:261
  408.8 36.9 %collective-permute-start.9 = (bf16[1,32,1024]{2,1,0:T(8,128)(2,1)S(1)}, bf16[1,32,1024]{2,1,0:T(8,128)(2,1)S(1)}, u32[]{:S(2)}, u32[]{:S(2)}) collective-permute-start(bf16[1,32,1024]{2,1,0:T(8,128)(2,1)S(1)} %copy-done.14), channel_id=1, source_target_pairs={{0,32},{32,64},{64,96},{96,128},{128,160},{160,192},{192,224},{224... | collective-permute-start | bytes 196616 | tf_op jit(solution)/shard_map/ppermute | solution.py:106
  (15 other events, 203.7 us)
Sparse Core Ops, SparseCore 0:
  15.9 68.8 all-gather.26
  169.5 14.8 all-gather.36
  186.2 37.2 all-gather.28
  225.1 29.6 all-gather.38
  256.5 20.8 all-gather.30
  279.0 57.6 all-gather.40
  338.5 65.6 all-gather.32
  408.8 71.4 all-gather.24
  482.2 63.8 all-gather.34
where the time goes:
time: 564 us; the launch traced here: 556 us
  waiting for transfers between devices  223 us (40%)
  local copies, waits for them, and re-layouts  130 us (23%)
  blocking collectives  52.9 us (9%)
  between operations  49.7 us (9%)
  matrix products  49.1 us (9%)
  other arithmetic  24.8 us (4%)
  starting transfers between devices  22.4 us (4%)
    dynamic_update_slice x2, local copies, waits for them, and re-layouts, layer_pair(): (local_state, ignored), mixed = lax.scan(span_update, start_carry, blocks)  50.9 us
    all_gather x1, waiting for transfers between devices, layer_pair(): lax.all_gather(w_mamba_in, CTX, axis=1, tiled=True)  50 us
    all_gather x1, waiting for transfers between devices, layer_pair(): lax.all_gather(w_qkv, CTX, axis=1, tiled=True)  39.8 us
    all_gather x3, waiting for transfers between devices, gathered_once(): both, at, found = (lax.all_gather(jnp.concatenate(lines), axis), 0, {})  37.1 us
    all_gather x1, waiting for transfers between devices, in_one_piece(): lax.all_gather(both, axis, axis=dim, tiled=True)  33.9 us
    all_gather x1, blocking collectives, layer_pair(): lax.all_gather(segment, CTX, axis=0, tiled=True)  32.5 us
    all_gather x2, waiting for transfers between devices, all_blocks(): blocks = lax.all_gather(blocks, axes[k])  26.3 us
    ppermute x10, starting transfers between devices, from_behind(): return lax.ppermute(value, axis, pairs)  22.1 us
  transfers between devices with their start and end apart: 19, of which 10 were waited for; matrix products, arithmetic and copies ran while one was open for 20% of the time, Pallas kernels for 0%

commit v1 on v0

--- a/solution.py
+++ b/solution.py
@@ -15,6 +15,12 @@
 CTX = ("ctx_0", "ctx_1", "ctx_2")
 epsilon = 1e-05
 highest = lax.Precision.HIGHEST
+
+
+def write_figure(piece_in):
+    return jnp.concatenate(
+        lax.all_to_all(jnp.stack(lax.axis_size(CTX) * [piece_in], 0), CTX, 0, 0), axis=1
+    )
 
 
 def filled_with(value, identity):
@@ -210,9 +216,9 @@
         columns, whole_of(w_mamba_out, CTX, (1, 0, 2), 0), preferred_element_type=jnp.float32
     )
     hidden = rms_norm(first, norm_gain[1]).astype(jnp.bfloat16)
-    projected = jnp.dot(
-        hidden, lax.all_gather(w_qkv, CTX, axis=1, tiled=True), preferred_element_type=jnp.float32
-    ).astype(jnp.bfloat16)
+    projected = jnp.dot(hidden, write_figure(w_qkv), preferred_element_type=jnp.float32).astype(
+        jnp.bfloat16
+    )
     groups = QUERY_HEADS // KV_HEADS
     query = projected[:, : QUERY_HEADS * ATTN_DIM].reshape(rows, KV_HEADS, groups, ATTN_DIM)
     keys = projected[:, QUERY_HEADS * ATTN_DIM : (QUERY_HEADS + KV_HEADS) * ATTN_DIM]

time: 564 us -> 611 us (1.083)
  waiting for transfers between devices: 223 us -> 252 us
  starting transfers between devices: 22.4 us -> 39.5 us
    all_gather x3, waiting for transfers between devices: 37.1 us -> 103 us  [gathered_once(): both, at, found = (lax.all_gather(jnp.concatenate(lines), axis), 0, {})]
    all_gather x1 -> x0, waiting for transfers between devices: 39.8 us -> none  [layer_pair(): lax.all_gather(w_qkv, CTX, axis=1, tiled=True)]
    all_to_all x0 -> x1, starting transfers between devices: none -> 16.1 us  [write_figure(): lax.all_to_all(jnp.stack(lax.axis_size(CTX) * [piece_in], 0), CTX, 0, 0)]
  transfers between devices with their start and end apart: 19 -> 19, of which waited for: 10 -> 9; matrix products, arithmetic and copies ran while one was open for 20% -> 19% of each run, Pallas kernels for 0% -> 0%
where the time goes in v1:
time: 611 us; the launch traced here: 603 us
  waiting for transfers between devices  252 us (41%)
  local copies, waits for them, and re-layouts  132 us (22%)
  blocking collectives  52.2 us (9%)
  between operations  50.1 us (8%)
  matrix products  49.1 us (8%)
  starting transfers between devices  39.5 us (6%)
  other arithmetic  24.8 us (4%)
    all_gather x3, waiting for transfers between devices, gathered_once(): both, at, found = (lax.all_gather(jnp.concatenate(lines), axis), 0, {})  103 us
    dynamic_update_slice x2, local copies, waits for them, and re-layouts, layer_pair(): (local_state, ignored), mixed = lax.scan(span_update, start_carry, blocks)  50.9 us
    all_gather x1, waiting for transfers between devices, layer_pair(): lax.all_gather(w_mamba_in, CTX, axis=1, tiled=True)  49.9 us
    all_gather x1, waiting for transfers between devices, in_one_piece(): lax.all_gather(both, axis, axis=dim, tiled=True)  36.6 us
    all_gather x1, blocking collectives, layer_pair(): lax.all_gather(segment, CTX, axis=0, tiled=True)  31.9 us
    all_gather x2, waiting for transfers between devices, all_blocks(): blocks = lax.all_gather(blocks, axes[k])  26.4 us
    ppermute x10, starting transfers between devices, from_behind(): return lax.ppermute(value, axis, pairs)  23.1 us
    squeeze x12, local copies, waits for them, and re-layouts, entering_2(): so_far = combine(so_far, jax.tree.map(lambda part: part[k], pieces))  21.3 us
  transfers between devices with their start and end apart: 19, of which 9 were waited for; matrix products, arithmetic and copies ran while one was open for 19% of the time, Pallas kernels for 0%

profile of v1, /device:TPU:1, one launch (start us, length us, event | category | flops | bytes accessed | tf_op | source)
XLA Modules:
  0.0 602.5 jit_solution(11947317060796020577)
XLA Ops:
  10.1 5.0 collective-permute-done.4
  34.9 49.9 %all-gather.25.cloned.1.call-done = bf16[1,1024,2048]{1,2,0:T(8,128)(2,1)} async-done(((bf16[1,1024,64]{1,2,0:T(8,128)(2,1)}), bf16[1,1024,2048]{1,2,0:T(8,128)(2,1)}) %all-gather.25.cloned.1.call-update) | async-done | bytes 4194320 | tf_op jit(solution)/shard_map/all_gather | solution.py:174
  84.8 3.8 fusion.46
  90.8 76.3 %while.15 = (s32[]{:T(128)}, f32[32,64,64]{2,1,0:T(8,128)S(1)}, s32[]{:T(128)}, f32[2,64,32,64]{1,0,3,2:T(2,128)}, s32[2,64]{1,0:T(2,128)}, /*index=5*/f32[2,64,...) while((s32[]{:T(128)}, f32[32,64,64]{2,1,0:T(8,128)S(1)}, ...), condition=%wide.region_3.4_spmd.clone, body=%wide.region_1.3_spmd.clone.sunk | while | flops 306858144 | bytes 9277010 | solution.py:190
  102.9 25.5 %dynamic_update_slice.6 = f32[2,64,32,64]{1,0,3,2:T(2,128)} dynamic-update-slice(f32[2,64,32,64]{1,0,3,2:T(2,128)} %get-tuple-element.314, f32[1,64,32,64]{1,0,3,2:T(1,128)S(1)} %bitcast.295, s32[]{:T(128)S(6)} %copy.186, s32[]{:T(128)} %constant.29.clone.1..sunk, s32[]{:T(128)} %constant.29.clone.1..sunk, s32[]{:T(128)} %constant.29.clone.1..sunk) | dynamic-update-slice | bytes 1048580 | tf_op jit(solution)/shard_map/while/body/jit(dynamic_update_index_in_dim)/dynamic_update_slice | solution.py:190
  141.1 25.5 %dynamic_update_slice.6 = f32[2,64,32,64]{1,0,3,2:T(2,128)} dynamic-update-slice(f32[2,64,32,64]{1,0,3,2:T(2,128)} %get-tuple-element.314, f32[1,64,32,64]{1,0,3,2:T(1,128)S(1)} %bitcast.295, s32[]{:T(128)S(6)} %copy.186, s32[]{:T(128)} %constant.29.clone.1..sunk, s32[]{:T(128)} %constant.29.clone.1..sunk, s32[]{:T(128)} %constant.29.clone.1..sunk) | dynamic-update-slice | bytes 1048580 | tf_op jit(solution)/shard_map/while/body/jit(dynamic_update_index_in_dim)/dynamic_update_slice | solution.py:190
  171.9 6.0 collective-permute-done.7
  177.9 4.6 all_gather.76
  196.9 26.4 %all-gather.27.cloned.1.call-done = bf16[16,64,1024]{2,1,0:T(8,128)(2,1)} async-done(((bf16[2,64,1024]{2,1,0:T(8,128)(2,1)}), bf16[16,64,1024]{2,1,0:T(8,128)(2,1)}) %all-gather.27.cloned.1.call-update) | async-done | bytes 2097168 | tf_op jit(solution)/shard_map/all_gather | solution.py:89
  239.5 8.9 %all-reduce.5 = s32[16]{0:T(128)S(1)} all-reduce(s32[16]{0:T(128)S(1)} %fusion.169), channel_id=5, replica_groups=mesh['blk'=8,'ctx_0'=8,'ctx_1'=2,'ctx_2'=2] {'ctx_0'}, use_global_device_ids=true, to_apply=%add.5 | all-reduce | flops 16 | bytes 128
  267.0 4.7 collective-permute-done.8
  274.4 16.1 %all-to-all-start = ((bf16[32,1024,64]{1,2,0:T(8,128)(2,1)}), bf16[32,1024,64]{1,2,0:T(8,128)(2,1)}, u32[]{:S(2)}, u32[]{:S(2)}) async-start(bf16[32,1024,64]{1,2,0:T(8,128)(2,1)} %stack.3), calls=%async_computation | async-start | bytes 8388608 | tf_op jit(solution)/shard_map/all_to_all | solution.py:22
  302.2 5.0 copy.122
  317.6 102.7 %all-gather.37.cloned.1.call-done = f32[8,2049,64]{1,2,0:T(8,128)} async-done(((f32[1,2049,64]{1,2,0:T(8,128)}), f32[8,2049,64]{1,2,0:T(8,128)}) %all-gather.37.cloned.1.call-update) | async-done | bytes 4196368 | tf_op jit(solution)/shard_map/all_gather | solution.py:40
  440.1 6.5 %multiply_reduce_fusion = (f32[128]{0:T(128)S(1)}, f32[128,32,64]{0,2,1:T(8,128)S(1)}) fusion(f32[32]{0:T(128)S(1)} %bitcast_convert_fusion, f32[128,2048]{0,1:T(8,128)S(1)} %copy.121, f32[128,32,64]{0,2,1:T(8,128)S(1)} %copy-done.5, f32[128,32]{0,1:T(8,128)S(1)} %exponential_select_fusion.2, f32[32,64,64]{2,1,0:T(8,128)} %bitcast.297, ...), kind=kOutput, calls=%fused_computation.74 | convolution fusion | flops 207748992 | bytes 15780236 | tf_op jit(solution)/shard_map/tn,hpn->thp/dot_general | solution.py:205
  455.9 31.9 %all-gather.9 = s32[1,4096]{1,0:T(1,128)S(1)} all-gather(s32[1,128]{1,0:T(1,128)S(1)} %copy-done.11), channel_id=11, replica_groups=mesh['blk'=8,'ctx_0'=8,'ctx_1'=2,'ctx_2'=2] {'ctx_0','ctx_1','ctx_2'}, dimensions={1}, use_global_device_ids=true | all-gather | bytes 16896 | tf_op jit(solution)/shard_map/all_gather | solution.py:231
  490.5 36.6 %all-gather.23.cloned.1.call-done = bf16[4096,1024]{1,0:T(8,128)(2,1)} async-done(((bf16[128,1024]{1,0:T(8,128)(2,1)}), bf16[4096,1024]{1,0:T(8,128)(2,1)}) %all-gather.23.cloned.1.call-update) | async-done | bytes 8388624 | tf_op jit(solution)/shard_map/all_gather | solution.py:106
  527.1 5.8 fusion.177
  532.9 7.0 %reshape.507 = bf16[4096,4,128]{2,1,0:T(4,128)(2,1)} reshape(bf16[4096,512]{1,0:T(8,128)(2,1)} %get-tuple-element.166) | data formatting | bytes 8388608 | tf_op jit(solution)/shard_map/reshape | solution.py:239
  539.9 9.8 %fusion.33 = (f32[4,2,128]{2,1,0:T(2,128)S(1)}, f32[4,4096,128,2]{2,1,3,0:T(8,128)}) fusion(pred[128,4096]{0,1:T(8,128)(4,1)S(1)} %fusion.51, bf16[128,4,2,128]{3,2,1,0:T(2,128)(2,1)S(1)} %reshape.508, bf16[4096,4,128,1]{2,1,0,3:T(4,128)(2,1)} %bitcast.311), kind=kOutput, calls=%fused_computation.50 | convolution fusion | flops 1086323712 | bytes 21762048 | tf_op jit(solution)/shard_map/tkgd,skd->kgts/dot_general | solution.py:236
  549.6 6.5 %copy.150 = bf16[4096,512]{0,1:T(8,128)(2,1)} copy(bf16[4096,512]{1,0:T(8,128)(2,1)} %get-tuple-element.167) | data formatting | bytes 8388608 | tf_op jit(solution)/shard_map/reshape | solution.py:254
  556.1 8.2 %fusion.34 = f32[4,2,128]{2,1,0:T(2,128)S(1)} fusion(f32[4,4096,128,2]{2,1,3,0:T(8,128)} %get-tuple-element.226, f32[4,2,128]{2,1,0:T(2,128)S(1)} %broadcast_maximum_fusion, pred[128,4096]{0,1:T(8,128)(4,1)S(1)} %fusion.51), kind=kLoop, calls=%fused_computation.51 | loop fusion | flops 20970496 | bytes 17309696 | tf_op jit(solution)/shard_map/reduce_sum | solution.py:250
  566.9 6.5 %fusion.105 = bf16[128,4,2,128]{0,3,2,1:T(8,128)(2,1)S(1)} fusion(bf16[4096,4,128,1]{0,2,3,1:T(8,128)(2,1)} %bitcast.310, f32[4,4096,128,2]{2,1,3,0:T(8,128)S(1)} %copy-done, f32[4,2,128]{2,1,0:T(2,128)S(1)} %broadcast_maximum_fusion, pred[128,4096]{0,1:T(8,128)(4,1)S(1)} %fusion.51, f32[128,4,2]{0,2,1:T(2,128)S(1)} %bitcast.327), kind=kOutput, calls=%fused_computation.114 | convolution fusion | flops 1094975488 | bytes 21766144 | tf_op jit(solution)/shard_map/kgts,skd->kgtd/dot_general | solution.py:251
  573.4 19.3 %all-gather.31.cloned.1.call-done = bf16[1,1024,1024]{2,1,0:T(8,128)(2,1)} async-done(((bf16[1,32,1024]{2,1,0:T(8,128)(2,1)}), bf16[1,1024,1024]{2,1,0:T(8,128)(2,1)}) %all-gather.31.cloned.1.call-update) | async-done | bytes 2097168 | tf_op jit(solution)/shard_map/all_gather | solution.py:267
  (213 shorter events, 127.9 us)
Async XLA Ops:
  6.5 78.3 %all-gather.25.cloned.1.call-start = ((), (), s32[]{:S(2)}) async-start(), calls=%async_computation.2 | async-start | bytes 4325376 | tf_op jit(solution)/shard_map/all_gather | solution.py:174
  6.5 8.6 %collective-permute-start.4 = (bf16[1,1024,64]{1,2,0:T(8,128)(2,1)}, bf16[1,1024,64]{1,2,0:T(8,128)(2,1)S(1)}, u32[]{:S(2)}, u32[]{:S(2)}) collective-permute-start(bf16[1,1024,64]{1,2,0:T(8,128)(2,1)} %param.17), channel_id=1, source_target_pairs={{0,32},{32,64},{64,96},{96,128},{128,160},{160,192},{192,224},{224... | collective-permute-start | bytes 393224 | tf_op jit(solution)/shard_map/ppermute | solution.py:112
  15.8 177.5 %all-gather.33.cloned.1.call-start = ((), (), s32[]{:S(2)}) async-start(), calls=%async_computation.6 | async-start | bytes 1671168 | tf_op jit(solution)/shard_map/all_gather | solution.py:40
  15.8 14.7 %collective-permute-start = (bf16[1,2,1024]{2,1,0:T(2,128)(2,1)}, bf16[1,2,1024]{2,1,0:T(2,128)(2,1)S(1)}, u32[]{:S(2)}, u32[]{:S(2)}) collective-permute-start(bf16[1,2,1024]{2,1,0:T(2,128)(2,1)} %param.16), channel_id=1, source_target_pairs={{0,32},{32,64},{64,96},{96,128},{128,160},{160,192},{192,224},{224... | collective-permute-start | bytes 12296 | tf_op jit(solution)/shard_map/ppermute | solution.py:112
  17.0 13.5 %collective-permute-start.3 = (bf16[1,32]{1,0:T(2,128)(2,1)}, bf16[1,32]{1,0:T(2,128)(2,1)S(1)}, u32[]{:S(2)}, u32[]{:S(2)}) collective-permute-start(bf16[1,32]{1,0:T(2,128)(2,1)} %param.19), channel_id=1, source_target_pairs={{0,32},{32,64},{64,96},{96,128},{128,160},{160,192},{192,224},{224... | collective-permute-start | bytes 200 | tf_op jit(solution)/shard_map/ppermute | solution.py:112
  19.1 11.4 %collective-permute-start.2 = (bf16[1,32]{1,0:T(2,128)(2,1)}, bf16[1,32]{1,0:T(2,128)(2,1)S(1)}, u32[]{:S(2)}, u32[]{:S(2)}) collective-permute-start(bf16[1,32]{1,0:T(2,128)(2,1)} %param.20), channel_id=1, source_target_pairs={{0,32},{32,64},{64,96},{96,128},{128,160},{160,192},{192,224},{224... | collective-permute-start | bytes 200 | tf_op jit(solution)/shard_map/ppermute | solution.py:112
  21.0 11.2 %collective-permute-start.1 = (bf16[1,1024,160]{1,2,0:T(8,128)(2,1)}, bf16[1,1024,160]{1,2,0:T(8,128)(2,1)S(1)}, u32[]{:S(2)}, u32[]{:S(2)}) collective-permute-start(bf16[1,1024,160]{1,2,0:T(8,128)(2,1)} %param.18), channel_id=1, source_target_pairs={{0,32},{32,64},{64,96},{96,128},{128,160},{160,192},{192,224},{224... | collective-permute-start | bytes 983048 | tf_op jit(solution)/shard_map/ppermute | solution.py:112
  167.5 57.3 %copy-start.17 = (u32[256]{0:T(256)S(1)}, u32[256]{0:T(256)}, u32[]{:S(2)}) copy-start(u32[256]{0:T(256)} %constant.109) | copy-start | bytes 3076
  167.5 67.2 %copy-start.16 = (u32[256]{0:T(256)S(1)}, u32[256]{0:T(256)}, u32[]{:S(2)}) copy-start(u32[256]{0:T(256)} %constant.114) | copy-start | bytes 3076
  169.2 54.1 %all-gather.27.cloned.1.call-start = ((), (), s32[]{:S(2)}) async-start(), calls=%async_computation.3 | async-start | bytes 2359296 | tf_op jit(solution)/shard_map/all_gather | solution.py:89
  169.3 8.7 %collective-permute-start.7 = (bf16[1,64,1024]{2,1,0:T(8,128)(2,1)}, bf16[1,64,1024]{2,1,0:T(8,128)(2,1)S(1)}, u32[]{:S(2)}, u32[]{:S(2)}) collective-permute-start(bf16[1,64,1024]{2,1,0:T(8,128)(2,1)} %param.23), channel_id=1, source_target_pairs={{0,32},{32,64},{64,96},{96,128},{128,160},{160,192},{192,224},{224... | collective-permute-start | bytes 393224 | tf_op jit(solution)/shard_map/ppermute | solution.py:112
  182.5 78.0 %all-gather.35.cloned.1.call-start = ((), (), s32[]{:S(2)}) async-start(), calls=%async_computation.7 | async-start | bytes 1671168 | tf_op jit(solution)/shard_map/all_gather | solution.py:40
  194.7 69.4 %copy-start.12 = (bf16[1,1024,64]{1,2,0:T(8,128)(2,1)S(1)}, bf16[1,1024,64]{1,2,0:T(8,128)(2,1)}, u32[]{:S(2)}) copy-start(bf16[1,1024,64]{1,2,0:T(8,128)(2,1)} %param.24) | copy-start | bytes 393220
  196.9 105.3 %all-gather.29.cloned.1.call-start = ((), (), s32[]{:S(2)}) async-start(), calls=%async_computation.4 | async-start | bytes 6291456 | tf_op jit(solution)/shard_map/all_gather | solution.py:89
  223.3 197.0 %all-gather.37.cloned.1.call-start = ((), (), s32[]{:S(2)}) async-start(), calls=%async_computation.8 | async-start | bytes 5013504 | tf_op jit(solution)/shard_map/all_gather | solution.py:40
  264.1 7.7 %collective-permute-start.8 = (bf16[1,1024,64]{1,2,0:T(8,128)(2,1)S(1)}, bf16[1,1024,64]{1,2,0:T(8,128)(2,1)S(1)}, u32[]{:S(2)}, u32[]{:S(2)}) collective-permute-start(bf16[1,1024,64]{1,2,0:T(8,128)(2,1)S(1)} %copy-done.12), channel_id=1, source_target_pairs={{0,32},{32,64},{64,96},{96,128},{128,160},{160,192},{192,224},{224... | collective-permute-start | bytes 393224 | tf_op jit(solution)/shard_map/ppermute | solution.py:112
  274.4 16.5 %copy-start.15 = (bf16[1,32]{1,0:T(2,128)(2,1)S(1)}, bf16[1,32]{1,0:T(2,128)(2,1)}, u32[]{:S(2)}) copy-start(bf16[1,32]{1,0:T(2,128)(2,1)} %param.21) | copy-start | bytes 196
  274.4 27.5 %copy-start.11 = (s32[1,128]{1,0:T(1,128)S(1)}, s32[1,128]{1,0:T(1,128)}, u32[]{:S(2)}) copy-start(s32[1,128]{1,0:T(1,128)} %param.15) | copy-start | bytes 1540
  274.4 173.5 %all-to-all-start = ((bf16[32,1024,64]{1,2,0:T(8,128)(2,1)}), bf16[32,1024,64]{1,2,0:T(8,128)(2,1)}, u32[]{:S(2)}, u32[]{:S(2)}) async-start(bf16[32,1024,64]{1,2,0:T(8,128)(2,1)} %stack.3), calls=%async_computation | async-start | bytes 8388608 | tf_op jit(solution)/shard_map/all_to_all | solution.py:22
  290.5 236.6 %all-gather.23.cloned.1.call-start = ((), (), s32[]{:S(2)}) async-start(), calls=%async_computation.1 | async-start | bytes 8650752 | tf_op jit(solution)/shard_map/all_gather | solution.py:106
  290.6 11.4 %collective-permute-start.6 = (bf16[1,2048]{1,0:T(2,128)(2,1)S(1)}, bf16[1,2048]{1,0:T(2,128)(2,1)S(1)}, u32[]{:S(2)}, u32[]{:S(2)}) collective-permute-start(bf16[1,2048]{1,0:T(2,128)(2,1)S(1)} %copy-done.14), channel_id=1, source_target_pairs={{0,32},{32,64},{64,96},{96,128},{128,160},{160,192},{192,224},{224... | collective-permute-start | bytes 12296 | tf_op jit(solution)/shard_map/ppermute | solution.py:112
  290.9 11.0 %collective-permute-start.5 = (bf16[1,32]{1,0:T(2,128)(2,1)S(1)}, bf16[1,32]{1,0:T(2,128)(2,1)S(1)}, u32[]{:S(2)}, u32[]{:S(2)}) collective-permute-start(bf16[1,32]{1,0:T(2,128)(2,1)S(1)} %copy-done.15), channel_id=1, source_target_pairs={{0,32},{32,64},{64,96},{96,128},{128,160},{160,192},{192,224},{224... | collective-permute-start | bytes 200 | tf_op jit(solution)/shard_map/ppermute | solution.py:112
  452.4 140.3 %all-gather.31.cloned.1.call-start = ((), (), s32[]{:S(2)}) async-start(), calls=%async_computation.5 | async-start | bytes 2162688 | tf_op jit(solution)/shard_map/all_gather | solution.py:267
  452.5 37.2 %collective-permute-start.9 = (bf16[1,32,1024]{2,1,0:T(8,128)(2,1)S(1)}, bf16[1,32,1024]{2,1,0:T(8,128)(2,1)S(1)}, u32[]{:S(2)}, u32[]{:S(2)}) collective-permute-start(bf16[1,32,1024]{2,1,0:T(8,128)(2,1)S(1)} %copy-done.13), channel_id=1, source_target_pairs={{0,32},{32,64},{64,96},{96,128},{128,160},{160,192},{192,224},{224... | collective-permute-start | bytes 196616 | tf_op jit(solution)/shard_map/ppermute | solution.py:112
  (14 other events, 82.3 us)
Sparse Core Ops, SparseCore 0:
  15.9 68.8 all-gather.24
  169.3 14.8 all-gather.32
  186.0 37.2 all-gather.26
  224.9 29.6 all-gather.34
  256.3 20.9 all-gather.28
  278.9 141.3 all-gather.36
  452.5 74.5 all-gather.22
  529.0 63.6 all-gather.30
